TPU v7x, 32 devices: a whole 2x2x4 slice. The times are simulated.
32 devices in a mesh: grp: 4 (over y, core), span: 8 (over z, x).
Axes of the slice: x: 2, y: 2, z: 4, core: 2. Of those that a mesh axis runs over, the one named last changes fastest.
Arguments:
- record: float32 [131072, 128], P(('grp', 'span')), may hold values from -96 to 96, as said below
Outputs:
- triangle: float32 [512, 512], replicated
- operator: float32 [512, 512], replicated
Inputs may be any that keep to these rules, and one draw needn't show every extreme that they name: `record`: Real-valued probe samples.
All inputs are finite; a program needn't handle non-finite values.
Results may differ from a plain program's by a relative error of at most 0.0003.
Values sent between devices are 32-bit elements; how exact they have to be, the bound alone decides.
A program may use at most 64 MiB of HBM per device.

v0:
```python
import jax
import jax.numpy as jnp
from jax import lax
from jax.sharding import PartitionSpec as P

LAGS = 4
DELAY = 1024


def shifted(value, axis, steps):
    count = lax.axis_size(axis)
    leading, last = (max(0, -steps), min(count, count - steps))
    return lax.ppermute(value, axis, [(source, source + steps) for source in range(leading, last)])


def inner_rows(left, right):
    return lax.dot_general(
        left,
        right,
        (((0,), (0,)), ((), ())),
        precision=lax.Precision.HIGHEST,
        preferred_element_type=jnp.float32,
    )


def on_device(record):
    count = record.shape[0]
    lead = (LAGS - 1) * DELAY + 1
    following = shifted(record[:lead], ("grp", "span"), -1)
    ext = jnp.concatenate([record, following], 0)
    hank = jnp.concatenate([ext[k * DELAY : k * DELAY + count + 1] for k in range(LAGS)], 1)
    devices = lax.axis_size(("grp", "span"))
    last_row = count * devices - lead
    times = lax.axis_index(("grp", "span")) * count + jnp.arange(count, dtype=jnp.int32)
    weight = (
        jnp.where(times < last_row, 1.0, 0.0)
        - 0.5 * jnp.where(times == 0, 1.0, 0.0)
        - 0.5 * jnp.where(times == last_row, 1.0, 0.0)
    )
    weight = weight.astype(jnp.float32)
    inside = jnp.where(times < last_row, 1.0, 0.0).astype(jnp.float32)
    head = hank[:count]
    weighted = head * weight[:, None]
    cross = inner_rows(head * inside[:, None], hank[1 : count + 1])
    scale = 1.0 / last_row
    gram = inner_rows(weighted, head)
    gram, cross = lax.psum((gram, cross), ("grp", "span"))
    lower = jnp.linalg.cholesky(gram * scale)
    middle = jax.scipy.linalg.solve_triangular(lower, cross * scale, lower=True)
    operator = jax.scipy.linalg.solve_triangular(lower, middle.T, lower=True).T
    return (lower.T, operator)


def solution(mesh):
    placed = (P(("grp", "span"), None),)
    return jax.shard_map(
        on_device, mesh=mesh, in_specs=placed, out_specs=(P(), P()), check_vma=False
    )
```

profile of v0, /device:TPU:0, one launch (start us, length us, event | category | flops | bytes accessed | tf_op | source)
XLA Modules:
  0.0 379.2 jit_solution(13203362706034608490)
XLA Ops:
  7.2 1.5 slice.124
  8.7 1.3 collective-permute-start
  10.0 1.7 constant_dynamic-update-slice_fusion.1
  11.8 36.3 %collective-permute-done = f32[3073,128]{1,0:T(8,128)S(1)} collective-permute-done((f32[3073,128]{1,0:T(8,128)S(1)}, f32[3073,128]{1,0:T(8,128)S(1)}, u32[]{:S(2)}, u32[]{:S(2)}) %collective-permute-start) | collective-permute-done | bytes 1573408 | tf_op jit(solution)/shard_map/ppermute | solution.py:13
  48.2 0.5 fusion.64
  48.7 1.4 pad_maximum_fusion
  50.1 17.3 %fusion.2 = f32[512,512]{0,1:T(8,128)} fusion(f32[4097,512]{1,0:T(8,128)S(1)} %pad_maximum_fusion, f32[4096]{0:T(1024)S(1)} %get-tuple-element.52), kind=kOutput, calls=%fused_computation.5 | convolution fusion | flops 12886999040 | bytes 17842176 | tf_op jit(solution)/shard_map/dot_general | solution.py:17
  67.4 16.4 %fusion = f32[512,512]{0,1:T(8,128)} fusion(f32[4097,512]{1,0:T(8,128)S(1)} %pad_maximum_fusion, f32[4096]{0:T(1024)S(1)} %get-tuple-element.51), kind=kOutput, calls=%fused_computation.2 | convolution fusion | flops 12886999040 | bytes 17842176 | tf_op jit(solution)/shard_map/dot_general | solution.py:17
  83.8 139.5 %all-reduce.4.cloned.1.call-done = (f32[512,512]{0,1:T(8,128)}, f32[512,512]{0,1:T(8,128)}) async-done(((f32[512,512]{0,1:T(8,128)}, f32[512,512]{0,1:T(8,128)}), (f32[512,512]{0,1:T(8,128)}, f32[512,512]{0,1:T(8,128)})) %all-reduce.4.cloned.1.call-update) | async-done | bytes 2097168 | tf_op jit(solution)/shard_map/psum | solution.py:47
  223.3 1.3 broadcast_multiply_fusion.1
  225.0 1.5 fusion.9
  226.5 11.7 %cholesky.104 = f32[128,128]{1,0:T(8,128)S(1)} custom-call(f32[128,128]{1,0:T(8,128)S(1)} %cholesky.266), custom_call_target="Cholesky" | custom-call | tf_op jit(solution)/shard_map/jit(cholesky)/cholesky | solution.py:48
  238.2 9.8 %custom-call.30 = f32[1,128,128]{1,2,0:T(8,128)S(1)} custom-call(f32[1,128,128]{2,1,0:T(8,128)S(1)} %get-tuple-element.48), custom_call_target="InvertDiagBlocksLowerTriangular" | custom-call | tf_op jit(solution)/shard_map/jit(cholesky)/cholesky | solution.py:48
  248.8 12.2 %cholesky.217 = f32[128,128]{1,0:T(8,128)S(1)} custom-call(f32[128,128]{1,0:T(8,128)S(1)} %cholesky.270), custom_call_target="Cholesky" | custom-call | tf_op jit(solution)/shard_map/jit(cholesky)/cholesky | solution.py:48
  261.0 0.6 compare_reduce_fusion.2
  261.7 0.6 compare_reduce_fusion.3
  262.3 9.8 %custom-call.31 = f32[1,128,128]{1,2,0:T(8,128)S(1)} custom-call(f32[1,128,128]{2,1,0:T(8,128)S(1)} %get-tuple-element.45), custom_call_target="InvertDiagBlocksLowerTriangular" | custom-call | tf_op jit(solution)/shard_map/jit(cholesky)/cholesky | solution.py:48
  272.8 11.7 %cholesky.238 = f32[128,128]{1,0:T(8,128)S(1)} custom-call(f32[128,128]{1,0:T(8,128)S(1)} %cholesky.275), custom_call_target="Cholesky" | custom-call | tf_op jit(solution)/shard_map/jit(cholesky)/cholesky | solution.py:48
  284.5 0.7 compare_reduce_fusion.1
  285.2 9.8 %custom-call.32 = f32[1,128,128]{1,2,0:T(8,128)S(1)} custom-call(f32[1,128,128]{2,1,0:T(8,128)S(1)} %get-tuple-element.42), custom_call_target="InvertDiagBlocksLowerTriangular" | custom-call | tf_op jit(solution)/shard_map/jit(cholesky)/cholesky | solution.py:48
  295.7 11.9 %cholesky.255 = f32[128,128]{1,0:T(8,128)S(1)} custom-call(f32[128,128]{1,0:T(8,128)S(1)} %convolution_subtract_fusion.8), custom_call_target="Cholesky" | custom-call | tf_op jit(solution)/shard_map/jit(cholesky)/cholesky | solution.py:48
  307.6 0.6 compare_reduce_fusion
  311.0 8.0 %while.4 = (s32[]{:T(128)}, f32[512,512]{1,0:T(8,128)S(1)}, s32[4,2]{0,1:T(2,128)S(1)}, f32[4,128,128]{2,1,0:T(8,128)S(1)}, s32[]{:T(128)}) while((s32[]{:T(128)}, f32[512,512]{1,0:T(8,128)S(1)}, s32[4,2]{0,1:T(2,128)S(1)}, f32[4,128,128]{2,1,0:T(8,128)S(1)}, s32[]{:T(128)}) %tuple.41), condition=%wide.while_cond.clone, body=%wide.while_body.clone.sunk | while | flops 2 | bytes 131181 | solution.py:50
  311.1 0.5 fusion.75
  311.6 1.4 bitcast_dynamic-update-slice_fusion.2
  313.1 0.5 fusion.75
  313.6 1.4 bitcast_dynamic-update-slice_fusion.2
  315.1 0.5 fusion.75
  315.6 1.4 bitcast_dynamic-update-slice_fusion.2
  317.1 0.5 fusion.75
  317.6 1.4 bitcast_dynamic-update-slice_fusion.2
  319.0 39.3 %custom-call.35 = f32[4,128,128]{1,2,0:T(8,128)S(1)} custom-call(f32[4,128,128]{2,1,0:T(8,128)S(1)} %get-tuple-element.18), custom_call_target="InvertDiagBlocksLowerTriangular" | custom-call | tf_op jit(solution)/shard_map/jit(_solve_triangular)/triangular_solve | solution.py:50
  358.4 1.3 broadcast_multiply_fusion
  359.7 0.4 fusion.30
  360.2 0.6 convolution_subtract_fusion.3
  360.8 0.4 fusion.48
  361.2 1.0 convolution_subtract_fusion.2
  362.2 0.4 fusion.50
  362.6 1.5 convolution_subtract_fusion.5
  364.1 0.4 fusion.52
  364.6 0.4 fusion.28
  365.1 0.6 convolution_subtract_fusion.1
  365.7 0.4 fusion.47
  366.1 1.0 convolution_subtract_fusion
  367.5 1.5 convolution_subtract_fusion.4
  369.0 0.4 fusion.51
  369.5 1.3 copy.7
  370.8 1.3 copy.6
  (30 shorter events, 3.8 us)
Async XLA Ops:
  7.2 216.1 %all-reduce.4.cloned.1.call-start = ((), (), s32[]{:S(2)}) async-start(), calls=%async_computation | async-start | bytes 4194304 | tf_op jit(solution)/shard_map/psum | solution.py:47
  8.7 39.3 %collective-permute-start = (f32[3073,128]{1,0:T(8,128)S(1)}, f32[3073,128]{1,0:T(8,128)S(1)}, u32[]{:S(2)}, u32[]{:S(2)}) collective-permute-start(f32[3073,128]{1,0:T(8,128)S(1)} %slice.124), channel_id=1, source_target_pairs={{1,0},{2,1},{3,2},{4,3},{5,4},{6,5},{7,6},{8,7},{9,8},{10,9},{11,1... | collective-permute-start | bytes 4720136 | tf_op jit(solution)/shard_map/ppermute | solution.py:13
Sparse Core Ops, SparseCore 0:
  83.9 139.3 all-reduce.3
where the time goes:
time: 384 us; the launch traced here: 379 us
  waiting for transfers between devices  176 us (46%)
  other arithmetic  125 us (33%)
  matrix products  45 us (12%)
  between operations  17.1 us (4%)
  local copies, waits for them, and re-layouts  14.9 us (4%)
    psum x1, waiting for transfers between devices, on_device(): gram, cross = lax.psum((gram, cross), ('grp', 'span'))  140 us
    another operation x15, other arithmetic, on_device(): lower = jnp.linalg.cholesky(gram * scale)  79.7 us
    another operation x4, other arithmetic, on_device(): operator = jax.scipy.linalg.solve_triangular(lower, middle.T, lower=True).T  39.6 us
    ppermute x1, waiting for transfers between devices, shifted(): lax.ppermute(value, axis, [(source, source + steps) for source in range(l...  36.3 us
    dot_general x2, matrix products, inner_rows(): lax.dot_general(left, right, (((0,), (0,)), ((), ())), precision=lax.Prec...  33.6 us
    another operation x13, local copies, waits for them, and re-layouts, on_device(): operator = jax.scipy.linalg.solve_triangular(lower, middle.T, lower=True).T  7.92 us
  transfers between devices with their start and end apart: 2, of which 2 were waited for; matrix products, arithmetic and copies ran while one was open for 0% of the time, Pallas kernels for 0%

commit v1 on v0

--- a/solution.py
+++ b/solution.py
@@ -44,7 +44,7 @@
     cross = inner_rows(head * inside[:, None], hank[1 : count + 1])
     scale = 1.0 / last_row
     gram = inner_rows(weighted, head)
-    gram, cross = lax.psum((gram, cross), ("grp", "span"))
+    gram, cross = lax.psum(lax.psum((gram, cross), "span"), "grp")
     lower = jnp.linalg.cholesky(gram * scale)
     middle = jax.scipy.linalg.solve_triangular(lower, cross * scale, lower=True)
     operator = jax.scipy.linalg.solve_triangular(lower, middle.T, lower=True).T

time: 384 us -> 405 us (1.055)
  waiting for transfers between devices: 176 us -> 197 us
    psum x1 -> x2, waiting for transfers between devices: 140 us -> 160 us  [on_device(): gram, cross = lax.psum(lax.psum((gram, cross), 'span'), 'grp')]
  transfers between devices with their start and end apart: 2 -> 3, of which waited for: 2 -> 3; matrix products, arithmetic and copies ran while one was open for 0% -> 0% of each run, Pallas kernels for 0% -> 0%
where the time goes in v1:
time: 405 us; the launch traced here: 400 us
  waiting for transfers between devices  197 us (49%)
  other arithmetic  125 us (31%)
  matrix products  45.2 us (11%)
  between operations  17.2 us (4%)
  local copies, waits for them, and re-layouts  14.9 us (4%)
    psum x2, waiting for transfers between devices, on_device(): gram, cross = lax.psum(lax.psum((gram, cross), 'span'), 'grp')  160 us
    another operation x15, other arithmetic, on_device(): lower = jnp.linalg.cholesky(gram * scale)  79.4 us
    another operation x4, other arithmetic, on_device(): operator = jax.scipy.linalg.solve_triangular(lower, middle.T, lower=True).T  39.6 us
    ppermute x1, waiting for transfers between devices, shifted(): lax.ppermute(value, axis, [(source, source + steps) for source in range(l...  36.3 us
    dot_general x2, matrix products, inner_rows(): lax.dot_general(left, right, (((0,), (0,)), ((), ())), precision=lax.Prec...  33.8 us
  transfers between devices with their start and end apart: 3, of which 3 were waited for; matrix products, arithmetic and copies ran while one was open for 0% of the time, Pallas kernels for 0%

profile of v1, /device:TPU:0, one launch (start us, length us, event | category | flops | bytes accessed | tf_op | source)
XLA Modules:
  0.0 400.0 jit_solution(7018317131418238983)
XLA Ops:
  7.2 1.5 slice.124
  8.7 1.3 collective-permute-start
  10.0 1.7 constant_dynamic-update-slice_fusion.1
  11.8 36.3 %collective-permute-done = f32[3073,128]{1,0:T(8,128)S(1)} collective-permute-done((f32[3073,128]{1,0:T(8,128)S(1)}, f32[3073,128]{1,0:T(8,128)S(1)}, u32[]{:S(2)}, u32[]{:S(2)}) %collective-permute-start) | collective-permute-done | bytes 1573408 | tf_op jit(solution)/shard_map/ppermute | solution.py:13
  48.2 0.5 fusion.64
  48.7 1.4 pad_maximum_fusion
  50.1 17.3 %fusion.2 = f32[512,512]{0,1:T(8,128)} fusion(f32[4097,512]{1,0:T(8,128)S(1)} %pad_maximum_fusion, f32[4096]{0:T(1024)S(1)} %get-tuple-element.54), kind=kOutput, calls=%fused_computation.5 | convolution fusion | flops 12886999040 | bytes 17842176 | tf_op jit(solution)/shard_map/dot_general | solution.py:17
  67.4 16.5 %fusion = f32[512,512]{0,1:T(8,128)} fusion(f32[4097,512]{1,0:T(8,128)S(1)} %pad_maximum_fusion, f32[4096]{0:T(1024)S(1)} %get-tuple-element.53), kind=kOutput, calls=%fused_computation.2 | convolution fusion | flops 12886999040 | bytes 17842176 | tf_op jit(solution)/shard_map/dot_general | solution.py:17
  84.0 107.2 %all-reduce.6.cloned.1.call-done = (f32[512,512]{0,1:T(8,128)}, f32[512,512]{0,1:T(8,128)}) async-done(((f32[512,512]{0,1:T(8,128)}, f32[512,512]{0,1:T(8,128)}), (f32[512,512]{0,1:T(8,128)}, f32[512,512]{0,1:T(8,128)})) %all-reduce.6.cloned.1.call-update) | async-done | bytes 2097168 | tf_op jit(solution)/shard_map/psum | solution.py:47
  191.2 53.1 %all-reduce.8.cloned.1.call-done = (f32[512,512]{0,1:T(8,128)}, f32[512,512]{0,1:T(8,128)}) async-done(((f32[512,512]{0,1:T(8,128)}, f32[512,512]{0,1:T(8,128)}), (f32[512,512]{0,1:T(8,128)}, f32[512,512]{0,1:T(8,128)})) %all-reduce.8.cloned.1.call-update) | async-done | bytes 2097168 | tf_op jit(solution)/shard_map/psum | solution.py:47
  244.3 1.3 broadcast_multiply_fusion.1
  246.0 1.5 fusion.9
  247.5 11.7 %cholesky.104 = f32[128,128]{1,0:T(8,128)S(1)} custom-call(f32[128,128]{1,0:T(8,128)S(1)} %cholesky.266), custom_call_target="Cholesky" | custom-call | tf_op jit(solution)/shard_map/jit(cholesky)/cholesky | solution.py:48
  259.4 9.8 %custom-call.30 = f32[1,128,128]{1,2,0:T(8,128)S(1)} custom-call(f32[1,128,128]{2,1,0:T(8,128)S(1)} %get-tuple-element.50), custom_call_target="InvertDiagBlocksLowerTriangular" | custom-call | tf_op jit(solution)/shard_map/jit(cholesky)/cholesky | solution.py:48
  269.8 11.7 %cholesky.217 = f32[128,128]{1,0:T(8,128)S(1)} custom-call(f32[128,128]{1,0:T(8,128)S(1)} %cholesky.270), custom_call_target="Cholesky" | custom-call | tf_op jit(solution)/shard_map/jit(cholesky)/cholesky | solution.py:48
  281.6 0.6 compare_reduce_fusion.2
  282.2 0.6 compare_reduce_fusion.3
  282.9 9.9 %custom-call.31 = f32[1,128,128]{1,2,0:T(8,128)S(1)} custom-call(f32[1,128,128]{2,1,0:T(8,128)S(1)} %get-tuple-element.47), custom_call_target="InvertDiagBlocksLowerTriangular" | custom-call | tf_op jit(solution)/shard_map/jit(cholesky)/cholesky | solution.py:48
  293.5 11.7 %cholesky.238 = f32[128,128]{1,0:T(8,128)S(1)} custom-call(f32[128,128]{1,0:T(8,128)S(1)} %cholesky.275), custom_call_target="Cholesky" | custom-call | tf_op jit(solution)/shard_map/jit(cholesky)/cholesky | solution.py:48
  305.2 0.7 compare_reduce_fusion.1
  306.0 9.8 %custom-call.32 = f32[1,128,128]{1,2,0:T(8,128)S(1)} custom-call(f32[1,128,128]{2,1,0:T(8,128)S(1)} %get-tuple-element.44), custom_call_target="InvertDiagBlocksLowerTriangular" | custom-call | tf_op jit(solution)/shard_map/jit(cholesky)/cholesky | solution.py:48
  316.4 11.9 %cholesky.255 = f32[128,128]{1,0:T(8,128)S(1)} custom-call(f32[128,128]{1,0:T(8,128)S(1)} %convolution_subtract_fusion.8), custom_call_target="Cholesky" | custom-call | tf_op jit(solution)/shard_map/jit(cholesky)/cholesky | solution.py:48
  328.3 0.6 compare_reduce_fusion
  331.8 8.0 %while.4 = (s32[]{:T(128)}, f32[512,512]{1,0:T(8,128)S(1)}, s32[4,2]{0,1:T(2,128)S(1)}, f32[4,128,128]{2,1,0:T(8,128)S(1)}, s32[]{:T(128)}) while((s32[]{:T(128)}, f32[512,512]{1,0:T(8,128)S(1)}, s32[4,2]{0,1:T(2,128)S(1)}, f32[4,128,128]{2,1,0:T(8,128)S(1)}, s32[]{:T(128)}) %tuple.41), condition=%wide.while_cond.clone, body=%wide.while_body.clone.sunk | while | flops 2 | bytes 131181 | solution.py:50
  331.9 0.5 fusion.75
  332.4 1.4 bitcast_dynamic-update-slice_fusion.2
  333.9 0.5 fusion.75
  334.4 1.4 bitcast_dynamic-update-slice_fusion.2
  335.9 0.5 fusion.75
  336.4 1.4 bitcast_dynamic-update-slice_fusion.2
  337.9 0.5 fusion.75
  338.4 1.4 bitcast_dynamic-update-slice_fusion.2
  339.8 39.3 %custom-call.35 = f32[4,128,128]{1,2,0:T(8,128)S(1)} custom-call(f32[4,128,128]{2,1,0:T(8,128)S(1)} %get-tuple-element.18), custom_call_target="InvertDiagBlocksLowerTriangular" | custom-call | tf_op jit(solution)/shard_map/jit(_solve_triangular)/triangular_solve | solution.py:50
  379.1 1.3 broadcast_multiply_fusion
  380.5 0.4 fusion.30
  380.9 0.6 convolution_subtract_fusion.3
  381.5 0.4 fusion.48
  381.9 1.0 convolution_subtract_fusion.2
  383.4 1.5 convolution_subtract_fusion.5
  384.9 0.4 fusion.52
  385.4 0.4 fusion.28
  385.8 0.6 convolution_subtract_fusion.1
  386.4 0.4 fusion.47
  386.8 1.0 convolution_subtract_fusion
  388.3 1.5 convolution_subtract_fusion.4
  389.8 0.4 fusion.51
  390.3 1.3 copy.7
  391.6 1.3 copy.6
  (33 shorter events, 4.2 us)
Async XLA Ops:
  7.2 184.0 %all-reduce.6.cloned.1.call-start = ((), (), s32[]{:S(2)}) async-start(), calls=%async_computation | async-start | bytes 4194304 | tf_op jit(solution)/shard_map/psum | solution.py:47
  8.7 39.3 %collective-permute-start = (f32[3073,128]{1,0:T(8,128)S(1)}, f32[3073,128]{1,0:T(8,128)S(1)}, u32[]{:S(2)}, u32[]{:S(2)}) collective-permute-start(f32[3073,128]{1,0:T(8,128)S(1)} %slice.124), channel_id=1, source_target_pairs={{1,0},{2,1},{3,2},{4,3},{5,4},{6,5},{7,6},{8,7},{9,8},{10,9},{11,1... | collective-permute-start | bytes 4720136 | tf_op jit(solution)/shard_map/ppermute | solution.py:13
  83.9 160.4 %all-reduce.8.cloned.1.call-start = ((), (), s32[]{:S(2)}) async-start(), calls=%async_computation.1 | async-start | bytes 4194304 | tf_op jit(solution)/shard_map/psum | solution.py:47
Sparse Core Ops, SparseCore 0:
  84.1 107.0 all-reduce.5
  193.6 50.6 all-reduce.7
